TPU v7x, 32 devices: a whole 2x2x4 slice. The times are simulated.
32 devices in a mesh: pole: 4 (over x, core), row: 4 (over z), col: 2 (over y).
Axes of the slice: x: 2, y: 2, z: 4, core: 2. Of those that a mesh axis runs over, the one named last changes fastest.
Arguments:
- inverse: bfloat16 [4, 2, 6144, 6144], P('pole', None, 'col', 'row'), may hold values from -0.078125 to 0.078125
- factor: bfloat16 [4, 2, 6144, 512], P('pole', None, ('row', 'col')), may hold values from -6 to 6
- block_mask: int32 [2, 192], P(None, ('row', 'col')), may hold values from 0 to 1
- pole_real: float32 [4], P('pole'), may hold values from -1 to 1
- pole_imaginary: float32 [4], P('pole'), may hold values from -1 to 1
Outputs:
- density: bfloat16 [2, 4, 768, 512], P('col', 'row', 'pole')
All inputs are finite; a program needn't handle non-finite values.
Results may differ from a plain program's by a relative error of at most 0.0012.
Values may be sent and summed in bfloat16 or wider, within the bound.
A program may use at most 64 MiB of HBM per device.

v0:
```python
import jax
import jax.numpy as jnp
from jax import lax
from jax.sharding import PartitionSpec as P

W = 256
BLK = 32


def shards(inverse, factor, block_mask, pole_real, pole_imaginary):
    row_mask = jnp.repeat(block_mask.T, BLK, axis=0)
    column_mask = jnp.repeat(row_mask, W, axis=1).astype(jnp.bfloat16)
    masked = factor[0] * column_mask[None]
    inverse_real = inverse[0, 0]
    inverse_imaginary = inverse[0, 1]
    height = inverse_real.shape[0]
    columns_all = masked.shape[2]
    piece = lax.all_gather(masked, "col", axis=1, tiled=True)
    running_real = jnp.dot(inverse_real, piece[0], preferred_element_type=jnp.float32) - jnp.dot(
        inverse_imaginary, piece[1], preferred_element_type=jnp.float32
    )
    running_imaginary = jnp.dot(
        inverse_real, piece[1], preferred_element_type=jnp.float32
    ) + jnp.dot(inverse_imaginary, piece[0], preferred_element_type=jnp.float32)
    weight_real = pole_real[0]
    weight_imaginary = pole_imaginary[0]
    weighted = weight_real * running_real - weight_imaginary * running_imaginary
    row_count = lax.axis_size("row")
    pole_count = lax.axis_size("pole")
    owned = height // (row_count * pole_count)
    reordered = (
        weighted.reshape(row_count, pole_count, owned, columns_all)
        .transpose(1, 0, 2, 3)
        .reshape(height, columns_all)
    )
    density = lax.psum_scatter(reordered, ("pole", "row"), scatter_dimension=0, tiled=True)
    return density.reshape(1, 1, density.shape[0], columns_all).astype(jnp.bfloat16)


def solution(mesh):
    return jax.shard_map(
        shards,
        mesh=mesh,
        in_specs=(
            P("pole", None, "col", "row"),
            P("pole", None, ("row", "col"), None),
            P(None, ("row", "col")),
            P("pole"),
            P("pole"),
        ),
        out_specs=P("col", "row", "pole", None),
        check_vma=False,
    )
```

profile of v0, /device:TPU:0, one launch (start us, length us, event | category | flops | bytes accessed | tf_op | source)
XLA Modules:
  0.0 205.3 jit_solution(15061561385486198886)
XLA Ops:
  6.5 0.0 all-gather.2.cloned.1.call-start
  6.5 0.7 convert_bitcast_fusion.1
  7.2 0.1 copy.10
  7.4 1.0 broadcast_in_dim.8
  8.3 0.2 copy.13
  8.5 2.8 %bitcast_multiply_fusion = bf16[2,768,512]{2,1,0:T(8,128)(2,1)} fusion(bf16[1,2,768,512]{3,2,1,0:T(8,128)(2,1)} %param.6, bf16[768,512]{1,0:T(8,128)(2,1)S(1)} %bitcast.42), kind=kLoop, calls=%fused_computation.15 | loop fusion | flops 786432 | bytes 3932160 | tf_op jit(solution)/shard_map/mul | solution.py:13
  11.3 0.0 all-gather.2.cloned.1.call-update
  11.3 0.0 reduce-scatter.2.cloned.1.call-start
  12.7 46.4 %all-gather.2.cloned.1.call-done = bf16[2,1536,512]{2,1,0:T(8,128)(2,1)} async-done(((bf16[2,768,512]{2,1,0:T(8,128)(2,1)}), bf16[2,1536,512]{2,1,0:T(8,128)(2,1)}) %all-gather.2.cloned.1.call-update) | async-done | bytes 3145744 | tf_op jit(solution)/shard_map/all_gather | solution.py:18
  59.1 8.3 %fusion.4 = f32[512,3072]{1,0:T(8,128)S(1)} fusion(bf16[1,2,3072,1536]{3,2,1,0:T(8,128)(2,1)} %param.5, bf16[2,1536,512]{2,1,0:T(8,128)(2,1)} %all-gather.2.cloned.1.call-done), kind=kOutput, calls=%fused_computation.4 | convolution fusion | flops 4831838208 | bytes 17301504 | tf_op jit(solution)/shard_map/dot_general | solution.py:22
  67.4 0.0 copy-done
  67.5 0.0 slice-start.3
  67.5 0.0 slice-start.4
  67.5 10.9 %fusion = f32[512,3072]{1,0:T(8,128)} fusion(bf16[1,2,3072,1536]{3,2,1,0:T(8,128)(2,1)} %param.5, bf16[2,1536,512]{2,1,0:T(8,128)(2,1)S(1)} %copy-done), kind=kOutput, calls=%fused_computation | convolution fusion | flops 4831838208 | bytes 17301504 | tf_op jit(solution)/shard_map/dot_general | solution.py:24
  78.4 0.0 slice-done.2
  78.4 0.0 slice-done.3
  78.4 0.0 slice-done.4
  78.4 7.0 %fusion.2 = f32[512,3072]{1,0:T(8,128)} fusion(bf16[1,2,3072,1536]{3,2,1,0:T(8,128)(2,1)S(1)} %bitcast.45, bf16[2,1536,512]{2,1,0:T(8,128)(2,1)S(1)} %copy-done), kind=kOutput, calls=%fused_computation.2 | convolution fusion | flops 4831838208 | bytes 17301504 | tf_op jit(solution)/shard_map/dot_general | solution.py:19
  85.4 13.2 %subtract_bitcast_fusion = f32[3072,512]{0,1:T(8,128)} fusion(f32[512,3072]{1,0:T(8,128)S(1)} %fusion.4, f32[512,3072]{1,0:T(8,128)} %fusion, f32[512,3072]{1,0:T(8,128)} %fusion.2, bf16[1,2,3072,1536]{3,2,1,0:T(8,128)(2,1)} %param.5, f32[]{:T(128)} %bitcast.38, f32[]{:T(128)} %bitcast.37, bf16[2,1536,512]{2,1,0:T(8,128)(2,1)S(1)} %copy-done), kind=kOutput, calls=%fused_computation.12 | convolution fusion | flops 4839702528 | bytes 36176896 | tf_op jit(solution)/shard_map/dot_general | solution.py:19
  98.6 6.6 %copy.11 = f32[3072,512]{1,0:T(8,128)} copy(f32[3072,512]{0,1:T(8,128)} %subtract_bitcast_fusion) | data formatting | bytes 12582912 | tf_op jit(solution)/shard_map/sub | solution.py:27
  105.1 6.4 %copy.12 = f32[4,4,192,512]{3,2,1,0:T(8,128)} copy(f32[4,4,192,512]{3,2,0,1:T(8,128)} %bitcast.40) | data formatting | bytes 12582912 | tf_op jit(solution)/shard_map/transpose | solution.py:33
  111.5 0.0 reduce-scatter.2.cloned.1.call-update
  111.6 85.2 %reduce-scatter.2.cloned.1.call-done = f32[192,512]{1,0:T(8,128)} async-done(((f32[3072,512]{1,0:T(8,128)}), f32[192,512]{1,0:T(8,128)}) %reduce-scatter.2.cloned.1.call-update) | async-done | bytes 393232 | tf_op jit(solution)/shard_map/reduce_scatter | solution.py:36
  196.8 1.7 convert_bitcast_fusion
  (8 shorter events, 0.0 us)
Async XLA Ops:
  6.5 52.6 %all-gather.2.cloned.1.call-start = ((), (), s32[]{:S(2)}) async-start(), calls=%async_computation.1 | async-start | bytes 4718592 | tf_op jit(solution)/shard_map/all_gather | solution.py:18
  11.3 185.5 %reduce-scatter.2.cloned.1.call-start = ((), (), s32[]{:S(2)}) async-start(), calls=%async_computation.2 | async-start | bytes 6684672 | tf_op jit(solution)/shard_map/reduce_scatter | solution.py:36
  59.1 8.4 %copy-start = (bf16[2,1536,512]{2,1,0:T(8,128)(2,1)S(1)}, bf16[2,1536,512]{2,1,0:T(8,128)(2,1)}, u32[]{:S(2)}) copy-start(bf16[2,1536,512]{2,1,0:T(8,128)(2,1)} %all-gather.2.cloned.1.call-done) | copy-start | bytes 9437188
  59.1 19.3 %slice-start = ((s8[18874368]{0:T(1024)(128)(4,1)}), s8[4194304]{0:T(1024)(128)(4,1)S(1)}, s32[]{:S(2)}) async-start(s8[18874368]{0:T(1024)(128)(4,1)} %bitcast.44), calls=%async_computation.3 | async-start | bytes 8388608
  59.1 19.3 %slice-start.1 = ((s8[18874368]{0:T(1024)(128)(4,1)}), s8[4194304]{0:T(1024)(128)(4,1)S(1)}, s32[]{:S(2)}) async-start(s8[18874368]{0:T(1024)(128)(4,1)} %bitcast.44), calls=%async_computation.4 | async-start | bytes 8388608
  59.1 19.3 %slice-start.2 = ((s8[18874368]{0:T(1024)(128)(4,1)}), s8[4194304]{0:T(1024)(128)(4,1)S(1)}, s32[]{:S(2)}) async-start(s8[18874368]{0:T(1024)(128)(4,1)} %bitcast.44), calls=%async_computation.5 | async-start | bytes 8388608
  67.5 10.9 %slice-start.3 = ((s8[18874368]{0:T(1024)(128)(4,1)}), s8[4194304]{0:T(1024)(128)(4,1)S(1)}, s32[]{:S(2)}) async-start(s8[18874368]{0:T(1024)(128)(4,1)} %bitcast.44), calls=%async_computation.6 | async-start | bytes 8388608
  67.5 10.9 %slice-start.4 = ((s8[18874368]{0:T(1024)(128)(4,1)}), s8[2097152]{0:T(1024)(128)(4,1)S(1)}, s32[]{:S(2)}) async-start(s8[18874368]{0:T(1024)(128)(4,1)} %bitcast.44), calls=%async_computation.7 | async-start | bytes 4194304
Sparse Core Ops, SparseCore 0:
  11.4 47.6 all-gather.1
  111.7 85.0 reduce-scatter.1
where the time goes:
time: 206 us; the launch traced here: 205 us
  waiting for transfers between devices  132 us (64%)
  matrix products  39.4 us (19%)
  between operations  14.8 us (7%)
  local copies, waits for them, and re-layouts  14.3 us (7%)
  other arithmetic  5.14 us (2%)
    reduce_scatter x1, waiting for transfers between devices, shards(): lax.psum_scatter(reordered, ('pole', 'row'), scatter_dimension=0, tiled=T...  85.2 us
    all_gather x1, waiting for transfers between devices, shards(): piece = lax.all_gather(masked, 'col', axis=1, tiled=True)  46.4 us
    dot_general x1, matrix products, shards(): jnp.dot(inverse_real, piece[0], preferred_element_type=jnp.float32)  13.2 us
    dot_general x1, matrix products, shards(): jnp.dot(inverse_imaginary, piece[0], preferred_element_type=jnp.float32)  10.9 us
    dot_general x1, matrix products, shards(): jnp.dot(inverse_real, piece[1], preferred_element_type=jnp.float32)  8.33 us
    dot_general x1, matrix products, shards(): jnp.dot(inverse_imaginary, piece[1], preferred_element_type=jnp.float32)  6.97 us
    sub x1, local copies, waits for them, and re-layouts, shards(): weighted = weight_real * running_real - weight_imaginary * running_imaginary  6.56 us
    transpose x1, local copies, waits for them, and re-layouts, shards(): reordered = weighted.reshape(row_count, pole_count, owned, columns_all).t...  6.4 us
  transfers between devices with their start and end apart: 2, of which 2 were waited for; matrix products, arithmetic and copies ran while one was open for 0% of the time, Pallas kernels for 0%

commit v1 on v0

--- a/solution.py
+++ b/solution.py
@@ -1,13 +1,19 @@
+import functools
+
 import jax
 import jax.numpy as jnp
 from jax import lax
+from jax.experimental import pallas as pl
+from jax.experimental.pallas import tpu as pltpu
 from jax.sharding import PartitionSpec as P
 
 W = 256
 BLK = 32
-
-
-def shards(inverse, factor, block_mask, pole_real, pole_imaginary):
+LANES = 128
+MESH = pl.DeviceIdType.MESH
+
+
+def plain(inverse, factor, block_mask, pole_real, pole_imaginary):
     row_mask = jnp.repeat(block_mask.T, BLK, axis=0)
     column_mask = jnp.repeat(row_mask, W, axis=1).astype(jnp.bfloat16)
     masked = factor[0] * column_mask[None]
@@ -37,7 +43,313 @@
     return density.reshape(1, 1, density.shape[0], columns_all).astype(jnp.bfloat16)
 
 
+def kernel(
+    rows_n,
+    real_ref,
+    imaginary_ref,
+    mask_ref,
+    factor_ref,
+    inverse_ref,
+    out_ref,
+    a,
+    own_f,
+    far_f,
+    far_mask,
+    mask_wide,
+    rhs,
+    part,
+    core_in,
+    x_out,
+    x_in,
+    z_out,
+    z_in,
+    load_sem,
+    own_sem,
+    y_send,
+    y_recv,
+    m_send,
+    m_recv,
+    c_send,
+    c_recv,
+    x_send,
+    x_recv,
+    z_send,
+    z_recv,
+):
+    p = lax.axis_index("pole")
+    z = lax.axis_index("row")
+    y = lax.axis_index("col")
+    core = lax.rem(p, 2)
+    x = p // 2
+    sibling = {"pole": x * 2 + 1 - core}
+    across = {"pole": (1 - x) * 2 + core}
+    beside = {"col": 1 - y}
+    depth = factor_ref.shape[2]
+    chunks = far_f.shape[0]
+    owned = out_ref.shape[2]
+    pair = 2 * owned
+    group = 4 * owned
+    supers, blocks = mask_ref.shape
+    per_super = chunks // supers
+    steps = 2 * rows_n
+
+    barrier = pltpu.get_barrier_semaphore()
+    pl.semaphore_signal(barrier, inc=1, device_id=sibling, device_id_type=MESH)
+    pl.semaphore_signal(barrier, inc=1, device_id=across, device_id_type=MESH)
+    pl.semaphore_signal(barrier, inc=1, device_id=beside, device_id_type=MESH)
+    for d in range(1, rows_n):
+        pl.semaphore_signal(
+            barrier, inc=1, device_id={"row": lax.rem(z + d, rows_n)}, device_id_type=MESH
+        )
+
+    def row_of(j):
+        return lax.rem(z + 1 + lax.rem(j, rows_n), rows_n)
+
+    def half_of(j):
+        far = j < rows_n
+        return jnp.where(far, 1 - x, x)
+
+    def load(j):
+        rows = pl.ds(pl.multiple_of(row_of(j) * group + half_of(j) * pair, pair), pair)
+        return pltpu.make_async_copy(
+            inverse_ref.at[0, :, rows, :], a.at[:, rows, :], load_sem.at[j]
+        )
+
+    def own_copy(n):
+        return pltpu.make_async_copy(
+            factor_ref.at[0, :, :, pl.ds(n * LANES, LANES)], own_f.at[n], own_sem.at[n]
+        )
+
+    def gather(n):
+        return pltpu.make_async_remote_copy(
+            src_ref=factor_ref.at[0, :, :, pl.ds(n * LANES, LANES)],
+            dst_ref=far_f.at[n],
+            send_sem=y_send.at[n],
+            recv_sem=y_recv.at[n],
+            device_id=beside,
+            device_id_type=MESH,
+        )
+
+    masks = pltpu.make_async_remote_copy(
+        src_ref=mask_ref,
+        dst_ref=far_mask,
+        send_sem=m_send,
+        recv_sem=m_recv,
+        device_id=beside,
+        device_id_type=MESH,
+    )
+
+    def core_copy(n, j):
+        return pltpu.make_async_remote_copy(
+            src_ref=part.at[n, row_of(j), half_of(j), 1 - core],
+            dst_ref=core_in.at[n, j],
+            send_sem=c_send.at[n, j],
+            recv_sem=c_recv.at[n, j],
+            device_id=sibling,
+            device_id_type=MESH,
+        )
+
+    def x_copy(n, j):
+        return pltpu.make_async_remote_copy(
+            src_ref=x_out.at[n, j],
+            dst_ref=x_in.at[n, j],
+            send_sem=x_send.at[n, j],
+            recv_sem=x_recv.at[n, j],
+            device_id=across,
+            device_id_type=MESH,
+        )
+
+    def z_copy(n, d):
+        return pltpu.make_async_remote_copy(
+            src_ref=z_out.at[n, d],
+            dst_ref=z_in.at[n, d],
+            send_sem=z_send.at[n, d],
+            recv_sem=z_recv.at[n, d],
+            device_id={"row": lax.rem(z + 1 + d, rows_n)},
+            device_id_type=MESH,
+        )
+
+    for n in range(chunks):
+        own_copy(n).start()
+    pl.semaphore_wait(barrier, 3 + rows_n - 1)
+    masks.start()
+    for n in range(chunks):
+        gather(n).start()
+    for j in range(steps):
+        load(j).start()
+
+    def widen(half, ref):
+        values = ref[...].astype(jnp.float32)
+        row = lax.broadcasted_iota(jnp.int32, (depth, blocks), 0)
+        block = lax.broadcasted_iota(jnp.int32, (depth, blocks), 1)
+        low = block * (depth // blocks)
+        inside = jnp.logical_and(row >= low, row < low + depth // blocks)
+        for s in range(supers):
+            spread = jnp.where(inside, values[s : s + 1, :], 0.0)
+            column = jnp.sum(spread, axis=1, keepdims=True)
+            mask_wide[half, s] = jnp.broadcast_to(column, (depth, LANES)).astype(jnp.bfloat16)
+
+    widen(0, mask_ref)
+    masks.wait_recv()
+    widen(1, far_mask)
+    own_rows = pl.ds(pl.multiple_of(y * depth, depth), depth)
+    far_rows = pl.ds(pl.multiple_of((1 - y) * depth, depth), depth)
+    for n in range(chunks):
+        own_copy(n).wait()
+        for part_index in range(2):
+            rhs[n, own_rows, part_index * LANES : (part_index + 1) * LANES] = (
+                own_f[n, part_index] * mask_wide[0, n // per_super]
+            )
+    weight_real = real_ref[0]
+    weight_imaginary = imaginary_ref[0]
+
+    def send_x(n, j):
+        core_copy(n, j).wait_recv()
+        x_out[n, j] = part[n, row_of(j), half_of(j), core] + core_in[n, j]
+        x_copy(n, j).start()
+
+    def compute(n):
+        def body(j, carry):
+            if n == 0:
+                load(j).wait()
+            r = row_of(j)
+            h = half_of(j)
+            rows = pl.ds(pl.multiple_of(r * group + h * pair, pair), pair)
+            by_real = jnp.dot(a[0, rows, :], rhs[n], preferred_element_type=jnp.float32)
+            by_imaginary = jnp.dot(a[1, rows, :], rhs[n], preferred_element_type=jnp.float32)
+            real = by_real[:, :LANES] - by_imaginary[:, LANES:]
+            imaginary = by_real[:, LANES:] + by_imaginary[:, :LANES]
+            weighted = weight_real * real - weight_imaginary * imaginary
+            part[n, r, h] = weighted.reshape(2, owned, LANES)
+            core_copy(n, j).start()
+
+            @pl.when(jnp.logical_and(j >= 1, j <= rows_n))
+            def _():
+                send_x(n, j - 1)
+
+            return carry
+
+        lax.fori_loop(0, steps, body, 0)
+
+    def send_z(n):
+        def body(d, carry):
+            j = d + rows_n
+            core_copy(n, j).wait_recv()
+            x_copy(n, d).wait_recv()
+            z_out[n, d] = part[n, row_of(d), x, core] + core_in[n, j] + x_in[n, d]
+
+            @pl.when(d < rows_n - 1)
+            def _():
+                z_copy(n, d).start()
+
+            return carry
+
+        lax.fori_loop(0, rows_n, body, 0)
+
+    def finish(n):
+        total = z_out[n, rows_n - 1]
+        for d in range(rows_n - 1):
+            z_copy(n, d).wait_recv()
+            total = total + z_in[n, d]
+        out_ref[0, 0, :, n * LANES : (n + 1) * LANES] = total.astype(out_ref.dtype)
+
+    for n in range(chunks):
+        gather(n).wait_recv()
+        for part_index in range(2):
+            rhs[n, far_rows, part_index * LANES : (part_index + 1) * LANES] = (
+                far_f[n, part_index] * mask_wide[1, n // per_super]
+            )
+        compute(n)
+        if n >= 1:
+            send_z(n - 1)
+        if n >= 2:
+            finish(n - 2)
+    send_z(chunks - 1)
+    for n in range(max(chunks - 2, 0), chunks):
+        finish(n)
+
+    masks.wait_send()
+    for n in range(chunks):
+        gather(n).wait_send()
+
+        def drain(j, carry):
+            core_copy(n, j).wait_send()
+
+            @pl.when(j < rows_n)
+            def _():
+                x_copy(n, j).wait_send()
+
+            @pl.when(j < rows_n - 1)
+            def _():
+                z_copy(n, j).wait_send()
+
+            return carry
+
+        lax.fori_loop(0, steps, drain, 0)
+
+
+def fused(inverse, factor, block_mask, pole_real, pole_imaginary):
+    rows_n = lax.axis_size("row")
+    height, width = inverse.shape[2:]
+    depth, columns_all = factor.shape[2:]
+    chunks = columns_all // LANES
+    owned = height // (rows_n * 4)
+    f32 = jnp.float32
+    dma = pltpu.SemaphoreType.DMA
+    smem = pl.BlockSpec(memory_space=pltpu.SMEM)
+    vmem = pl.BlockSpec(memory_space=pltpu.VMEM)
+    anywhere = pl.BlockSpec(memory_space=pl.ANY)
+    return pl.pallas_call(
+        functools.partial(kernel, rows_n),
+        out_shape=jax.ShapeDtypeStruct((1, 1, owned, columns_all), jnp.bfloat16),
+        in_specs=[smem, smem, vmem, anywhere, anywhere],
+        out_specs=vmem,
+        scratch_shapes=[
+            pltpu.VMEM((2, height, width), jnp.bfloat16),
+            pltpu.VMEM((chunks, 2, depth, LANES), jnp.bfloat16),
+            pltpu.VMEM((chunks, 2, depth, LANES), jnp.bfloat16),
+            pltpu.VMEM(block_mask.shape, block_mask.dtype),
+            pltpu.VMEM((2, block_mask.shape[0], depth, LANES), jnp.bfloat16),
+            pltpu.VMEM((chunks, 2 * depth, 2 * LANES), jnp.bfloat16),
+            pltpu.VMEM((chunks, rows_n, 2, 2, owned, LANES), f32),
+            pltpu.VMEM((chunks, 2 * rows_n, owned, LANES), f32),
+            pltpu.VMEM((chunks, rows_n, owned, LANES), f32),
+            pltpu.VMEM((chunks, rows_n, owned, LANES), f32),
+            pltpu.VMEM((chunks, rows_n, owned, LANES), f32),
+            pltpu.VMEM((chunks, rows_n, owned, LANES), f32),
+            dma((2 * rows_n,)),
+            dma((chunks,)),
+            dma((chunks,)),
+            dma((chunks,)),
+            dma,
+            dma,
+            dma((chunks, 2 * rows_n)),
+            dma((chunks, 2 * rows_n)),
+            dma((chunks, rows_n)),
+            dma((chunks, rows_n)),
+            dma((chunks, rows_n)),
+            dma((chunks, rows_n)),
+        ],
+        compiler_params=pltpu.CompilerParams(
+            collective_id=0, has_side_effects=True, vmem_limit_bytes=60 * 1024 * 1024
+        ),
+    )(pole_real, pole_imaginary, block_mask, factor, inverse)
+
+
 def solution(mesh):
+    sizes = dict(mesh.shape)
+
+    def shards(inverse, factor, block_mask, pole_real, pole_imaginary):
+        supers = block_mask.shape[0]
+        wide = factor.shape[3] // supers
+        small = 2 * inverse.shape[2] * inverse.shape[3] * 2 <= 20 * 1024 * 1024
+        fits = sizes["pole"] == 4 and sizes["col"] == 2 and sizes["row"] >= 2
+        if fits and small and wide % LANES == 0:
+            body = fused
+        else:
+            body = plain
+        return body(inverse, factor, block_mask, pole_real, pole_imaginary)
+
     return jax.shard_map(
         shards,
         mesh=mesh,

time: 206 us -> 72 us (0.35)
  waiting for transfers between devices: 132 us -> 0 us
  Pallas kernels: 0 us -> 68.9 us
  matrix products: 39.4 us -> 0 us
  between operations: 14.8 us -> 1.3 us
  local copies, waits for them, and re-layouts: 14.3 us -> 1.62 us
  other arithmetic: 5.14 us -> 0 us
    reduce_scatter x1 -> x0, waiting for transfers between devices: 85.2 us -> none  [shards(): lax.psum_scatter(reordered, ('pole', 'row'), scatter_dimension=0, tiled=T...]
    pallas_call x0 -> x1, Pallas kernels: none -> 68.9 us  [fused(): pl.pallas_call(functools.partial(kernel, rows_n), out_shape=jax.ShapeDtyp...]
    all_gather x1 -> x0, waiting for transfers between devices: 46.4 us -> none  [shards(): piece = lax.all_gather(masked, 'col', axis=1, tiled=True)]
    dot_general x4 -> x0, matrix products: 39.4 us -> none  [the longest x1 13.2 us: shards(): jnp.dot(inverse_real, piece[0], preferred_element_type=jnp.float32)]
    sub x1 -> x0, local copies, waits for them, and re-layouts: 6.56 us -> none  [shards(): weighted = weight_real * running_real - weight_imaginary * running_imaginary]
    transpose x1 -> x0, local copies, waits for them, and re-layouts: 6.4 us -> none  [shards(): reordered = weighted.reshape(row_count, pole_count, owned, columns_all).t...]
    mul x1 -> x0, other arithmetic: 2.77 us -> none  [shards(): masked = factor[0] * column_mask[None]]
    convert_element_type x2 -> x0, other arithmetic: 2.38 us -> none  [the longest x1 1.7 us: shards(): density.reshape(1, 1, density.shape[0], columns_all).astype(jnp.bfloat16)]
  transfers between devices with their start and end apart: 2 -> 0, of which waited for: 2 -> 0; matrix products, arithmetic and copies ran while one was open for 0% -> 0% of each run, Pallas kernels for 0% -> 0%
where the time goes in v1:
time: 72 us; the launch traced here: 71.8 us
  Pallas kernels  68.9 us (96%)
  local copies, waits for them, and re-layouts  1.62 us (2%)
  between operations  1.3 us (2%)
    pallas_call x1, Pallas kernels, fused(): pl.pallas_call(functools.partial(kernel, rows_n), out_shape=jax.ShapeDtyp...  68.9 us
    unnamed x1, local copies, waits for them, and re-layouts  1.62 us

profile of v1, /device:TPU:0, one launch (start us, length us, event | category | flops | bytes accessed | tf_op | source)
XLA Modules:
  0.0 71.8 jit_solution(14792387736965689555)
XLA Ops:
  1.3 68.9 %shard_map.55 = bf16[1,1,192,512]{3,2,1,0:T(8,128)(2,1)} custom-call(f32[1]{0:T(128)S(6)} %copy.7.real_ref, f32[1]{0:T(128)S(6)} %copy.8.imaginary_ref, s32[2,24]{1,0:T(2,128)} %mask_ref.1, bf16[1,2,768,512]{3,2,1,0:T(8,128)(2,1)} %factor_ref.1, bf16[1,2,3072,1536]{3,2,1,0:T(8,128)(2,1)} %inverse_ref.1), custom_call_target="tpu_custom_call" | custom-call | tf_op jit(solution)/shard_map/pallas_call | solution.py:302
  70.2 1.6 %copy.9 = bf16[1,1,192,512]{3,2,1,0:T(8,128)(2,1)} copy(bf16[1,1,192,512]{3,2,1,0:T(8,128)(2,1)} %shard_map.55) | data formatting | bytes 393216

commit v2 on v1

--- a/solution.py
+++ b/solution.py
@@ -45,15 +45,18 @@
 
 def kernel(
     rows_n,
-    real_ref,
-    imaginary_ref,
-    mask_ref,
+    real_hbm,
+    imaginary_hbm,
+    mask_hbm,
     factor_ref,
     inverse_ref,
     out_ref,
     a,
     own_f,
     far_f,
+    real_ref,
+    imaginary_ref,
+    mask_ref,
     far_mask,
     mask_wide,
     rhs,
@@ -65,6 +68,7 @@
     z_in,
     load_sem,
     own_sem,
+    small_sem,
     y_send,
     y_recv,
     m_send,
@@ -102,8 +106,19 @@
             barrier, inc=1, device_id={"row": lax.rem(z + d, rows_n)}, device_id_type=MESH
         )
 
+    def partner(j):
+        step = rows_n - 1 - j
+        if rows_n & (rows_n - 1):
+            return lax.rem(z + rows_n - step, rows_n)
+        other = 0
+        bit = 1
+        while bit < rows_n:
+            other = other + bit * lax.rem(z // bit + step // bit, 2)
+            bit *= 2
+        return other
+
     def row_of(j):
-        return lax.rem(z + 1 + lax.rem(j, rows_n), rows_n)
+        return partner(lax.rem(j, rows_n))
 
     def half_of(j):
         far = j < rows_n
@@ -131,7 +146,7 @@
         )
 
     masks = pltpu.make_async_remote_copy(
-        src_ref=mask_ref,
+        src_ref=mask_hbm,
         dst_ref=far_mask,
         send_sem=m_send,
         recv_sem=m_recv,
@@ -165,10 +180,18 @@
             dst_ref=z_in.at[n, d],
             send_sem=z_send.at[n, d],
             recv_sem=z_recv.at[n, d],
-            device_id={"row": lax.rem(z + 1 + d, rows_n)},
+            device_id={"row": partner(d)},
             device_id_type=MESH,
         )
 
+    small = [
+        pltpu.make_async_copy(source, target, small_sem.at[i])
+        for i, (source, target) in enumerate(
+            ((mask_hbm, mask_ref), (real_hbm, real_ref), (imaginary_hbm, imaginary_ref))
+        )
+    ]
+    for copy in small:
+        copy.start()
     for n in range(chunks):
         own_copy(n).start()
     pl.semaphore_wait(barrier, 3 + rows_n - 1)
@@ -189,6 +212,8 @@
             column = jnp.sum(spread, axis=1, keepdims=True)
             mask_wide[half, s] = jnp.broadcast_to(column, (depth, LANES)).astype(jnp.bfloat16)
 
+    for copy in small:
+        copy.wait()
     widen(0, mask_ref)
     masks.wait_recv()
     widen(1, far_mask)
@@ -227,24 +252,34 @@
             def _():
                 send_x(n, j - 1)
 
+            if n >= 1:
+
+                @pl.when(jnp.logical_and(j >= 1, j <= rows_n - early))
+                def _():
+                    send_z(n - 1, early + j - 1)
+
             return carry
 
         lax.fori_loop(0, steps, body, 0)
 
-    def send_z(n):
+    early = rows_n // 2
+
+    def send_z(n, d):
+        j = d + rows_n
+        core_copy(n, j).wait_recv()
+        x_copy(n, d).wait_recv()
+        z_out[n, d] = part[n, row_of(d), x, core] + core_in[n, j] + x_in[n, d]
+
+        @pl.when(d < rows_n - 1)
+        def _():
+            z_copy(n, d).start()
+
+    def send_z_range(n, low, high):
         def body(d, carry):
-            j = d + rows_n
-            core_copy(n, j).wait_recv()
-            x_copy(n, d).wait_recv()
-            z_out[n, d] = part[n, row_of(d), x, core] + core_in[n, j] + x_in[n, d]
-
-            @pl.when(d < rows_n - 1)
-            def _():
-                z_copy(n, d).start()
-
+            send_z(n, d)
             return carry
 
-        lax.fori_loop(0, rows_n, body, 0)
+        lax.fori_loop(low, high, body, 0)
 
     def finish(n):
         total = z_out[n, rows_n - 1]
@@ -254,19 +289,21 @@
         out_ref[0, 0, :, n * LANES : (n + 1) * LANES] = total.astype(out_ref.dtype)
 
     for n in range(chunks):
+        if n >= 1:
+            send_z_range(n - 1, 0, early)
         gather(n).wait_recv()
         for part_index in range(2):
             rhs[n, far_rows, part_index * LANES : (part_index + 1) * LANES] = (
                 far_f[n, part_index] * mask_wide[1, n // per_super]
             )
         compute(n)
-        if n >= 1:
-            send_z(n - 1)
         if n >= 2:
             finish(n - 2)
-    send_z(chunks - 1)
-    for n in range(max(chunks - 2, 0), chunks):
-        finish(n)
+    send_z_range(chunks - 1, 0, early)
+    if chunks >= 2:
+        finish(chunks - 2)
+    send_z_range(chunks - 1, early, rows_n)
+    finish(chunks - 1)
 
     masks.wait_send()
     for n in range(chunks):
@@ -296,18 +333,20 @@
     owned = height // (rows_n * 4)
     f32 = jnp.float32
     dma = pltpu.SemaphoreType.DMA
-    smem = pl.BlockSpec(memory_space=pltpu.SMEM)
     vmem = pl.BlockSpec(memory_space=pltpu.VMEM)
     anywhere = pl.BlockSpec(memory_space=pl.ANY)
     return pl.pallas_call(
         functools.partial(kernel, rows_n),
         out_shape=jax.ShapeDtypeStruct((1, 1, owned, columns_all), jnp.bfloat16),
-        in_specs=[smem, smem, vmem, anywhere, anywhere],
+        in_specs=[anywhere] * 5,
         out_specs=vmem,
         scratch_shapes=[
             pltpu.VMEM((2, height, width), jnp.bfloat16),
             pltpu.VMEM((chunks, 2, depth, LANES), jnp.bfloat16),
             pltpu.VMEM((chunks, 2, depth, LANES), jnp.bfloat16),
+            pltpu.SMEM(pole_real.shape, f32),
+            pltpu.SMEM(pole_imaginary.shape, f32),
+            pltpu.VMEM(block_mask.shape, block_mask.dtype),
             pltpu.VMEM(block_mask.shape, block_mask.dtype),
             pltpu.VMEM((2, block_mask.shape[0], depth, LANES), jnp.bfloat16),
             pltpu.VMEM((chunks, 2 * depth, 2 * LANES), jnp.bfloat16),
@@ -319,6 +358,7 @@
             pltpu.VMEM((chunks, rows_n, owned, LANES), f32),
             dma((2 * rows_n,)),
             dma((chunks,)),
+            dma((3,)),
             dma((chunks,)),
             dma((chunks,)),
             dma,

time: 72 us -> 66.5 us (0.924)
  Pallas kernels: 68.9 us -> 63.5 us
    pallas_call x1, Pallas kernels: 68.9 us -> 63.5 us  [fused(): pl.pallas_call(functools.partial(kernel, rows_n), out_shape=jax.ShapeDtyp...]
where the time goes in v2:
time: 66.5 us; the launch traced here: 66.4 us
  Pallas kernels  63.5 us (95%)
  local copies, waits for them, and re-layouts  1.62 us (2%)
  between operations  1.3 us (2%)
    pallas_call x1, Pallas kernels, fused(): pl.pallas_call(functools.partial(kernel, rows_n), out_shape=jax.ShapeDtyp...  63.5 us
    unnamed x1, local copies, waits for them, and re-layouts  1.62 us

profile of v2, /device:TPU:0, one launch (start us, length us, event | category | flops | bytes accessed | tf_op | source)
XLA Modules:
  0.0 66.4 jit_solution(2064392733183286603)
XLA Ops:
  1.3 63.5 %shard_map.55 = bf16[1,1,192,512]{3,2,1,0:T(8,128)(2,1)} custom-call(f32[1]{0:T(128)S(6)} %copy.7.real_hbm, f32[1]{0:T(128)S(6)} %copy.8.imaginary_hbm, s32[2,24]{1,0:T(2,128)} %mask_hbm.1, bf16[1,2,768,512]{3,2,1,0:T(8,128)(2,1)} %factor_ref.1, bf16[1,2,3072,1536]{3,2,1,0:T(8,128)(2,1)} %inverse_ref.1), custom_call_target="tpu_custom_call" | custom-call | tf_op jit(solution)/shard_map/pallas_call | solution.py:338
  64.8 1.6 %copy.9 = bf16[1,1,192,512]{3,2,1,0:T(8,128)(2,1)} copy(bf16[1,1,192,512]{3,2,1,0:T(8,128)(2,1)} %shard_map.55) | data formatting | bytes 393216
